TPU v7x, 256 devices: a whole 4x4x8 slice. The times are simulated.
256 devices in a mesh: tile: 64 (over z, y_lo, x), mode: 4 (over y_hi, core).
Axes of the slice: x: 4, y: 4 (y_hi: 2, y_lo: 2; y = y_hi * 2 + y_lo), z: 8, core: 2. Of those that a mesh axis runs over, the one named last changes fastest.
Arguments:
- object_tiles: float32 [64, 2, 2, 256, 256], P('tile'), may hold values from -6 to 6
- object_previous: float32 [64, 2, 2, 256, 256], P('tile'), may hold values from -6 to 6
- probe: float32 [4, 8, 2, 256, 256], P(None, 'mode', None, 'tile'), may hold values from -2 to 2
- probe_previous: float32 [4, 8, 2, 256, 256], P(None, 'mode', None, 'tile'), may hold values from -6 to 6
- patterns: float32 [128, 256, 256], P('tile'), may hold values from 0 to 2
- offsets: int32 [2, 128], P(None, 'tile'), may hold values from 0 to 255
- scan_of_slot: int32 [128], P('tile'), may hold values from 0 to 3
- tile_load: int32 [64], P('tile'), may hold values from 1 to 2, as said below
- step_sizes: int32 [2], replicated, may hold values from 128 to 511
- object_norm_before: float32 [1], replicated, may hold values from 0.1 to 0.4
- probe_norm_before: float32 [1], replicated, may hold values from 12 to 64
Outputs:
- new_object: float32 [64, 2, 2, 256, 256], P('tile')
- object_direction: float32 [64, 2, 2, 256, 256], P('tile')
- new_probe: float32 [4, 8, 2, 256, 256], P(None, 'mode', None, 'tile')
- probe_direction: float32 [4, 8, 2, 256, 256], P(None, 'mode', None, 'tile')
Inputs may be any that keep to these rules, and one draw needn't show every extreme that they name: `tile_load`: every tile holds 1 to 2 used slots, and some tile holds exactly 2.
All inputs are finite; a program needn't handle non-finite values.
Results may differ from a plain program's by a relative error of at most 0.024.
Values may be sent and summed in bfloat16 or wider, within the bound.
No kernel may reach another device: no remote copies, remote signals or barrier semaphores. Data moves between devices by JAX's collectives and lax.ppermute only.
A program may use at most 64 MiB of HBM per device.

v0:
```python
import math
import jax
import jax.numpy as jnp
from jax import lax
from jax.sharding import PartitionSpec as P

TGX = 8
MODES = 8
SCAN_COUNT = 4
residual_weight = 2.0


def from_behind(block, axis, distance):
    devices = range(lax.axis_size(axis))
    route = [(i - distance, i) for i in devices if i - distance in devices]
    return lax.ppermute(block, axis, route)


def table_pair(width):
    index_row = jnp.arange(width, dtype=jnp.int32)
    product = index_row[:, None] * index_row[None, :] % width
    angle = product.astype(jnp.float32) * (2.0 * math.pi / width)
    factor = 1.0 / math.sqrt(width)
    cosine = (jnp.cos(angle) * factor).astype(jnp.bfloat16)
    sine = (-jnp.sin(angle) * factor).astype(jnp.bfloat16)
    index_free = jnp.where(index_row < width // 2, index_row, index_row - width).astype(jnp.float32)
    phase = (
        index_free[:, None] * index_free[:, None] + index_free[None, :] * index_free[None, :]
    ) * (math.pi / (4.0 * width))
    return (cosine, sine, jnp.cos(phase), jnp.sin(phase))


def right_product(left_data, table):
    return jnp.einsum("...jk,kl->...jl", left_data, table, preferred_element_type=jnp.float32)


def left_product(table, right_data):
    return jnp.einsum("ij,...jl->...il", table, right_data, preferred_element_type=jnp.float32)


def transform(wave_re, wave_im, tables, inverse):
    cosine = tables[0]
    sine = -tables[1] if inverse else tables[1]
    first_re = (right_product(wave_re, cosine) - right_product(wave_im, sine)).astype(jnp.bfloat16)
    first_im = (right_product(wave_re, sine) + right_product(wave_im, cosine)).astype(jnp.bfloat16)
    out_re = (left_product(cosine, first_re) - left_product(sine, first_im)).astype(jnp.bfloat16)
    out_im = (left_product(sine, first_re) + left_product(cosine, first_im)).astype(jnp.bfloat16)
    return (out_re, out_im)


def complex_times(first_re, first_im, second_re, second_im):
    first_portion = first_re.astype(jnp.float32)
    b_part = first_im.astype(jnp.float32)
    c_part = second_re.astype(jnp.float32)
    d_part = second_im.astype(jnp.float32)
    return (first_portion * c_part - b_part * d_part, first_portion * d_part + b_part * c_part)


def conj_times(first_re, first_im, second_re, second_im):
    first_portion = first_re.astype(jnp.float32)
    b_part = first_im.astype(jnp.float32)
    c_part = second_re.astype(jnp.float32)
    d_part = second_im.astype(jnp.float32)
    return (first_portion * c_part + b_part * d_part, first_portion * d_part - b_part * c_part)


def propagate(wave_re, wave_im, tables, adjoint):
    spec_re, spec_im = transform(wave_re, wave_im, tables, False)
    kernel_im = -tables[3] if adjoint else tables[3]
    moved_re, moved_im = complex_times(spec_re, spec_im, tables[2], kernel_im)
    return transform(moved_re.astype(jnp.bfloat16), moved_im.astype(jnp.bfloat16), tables, True)


def body(
    object_tiles,
    object_previous,
    probe,
    probe_previous,
    patterns,
    offsets,
    scan_of_slot,
    tile_load,
    step_sizes,
    object_norm_before,
    probe_norm_before,
):
    tile_count = lax.axis_size("tile")
    mode_count = lax.axis_size("mode")
    slots = patterns.shape[0]
    width = patterns.shape[1]
    layers = object_tiles.shape[1]
    tile_side = object_tiles.shape[3]
    scans = probe.shape[0]
    tables = table_pair(width)
    own_tile = object_tiles[0].astype(jnp.bfloat16)
    east_part = from_behind(own_tile, "tile", -1)
    upper = jnp.concatenate([own_tile, east_part], axis=3)
    lower = from_behind(upper, "tile", -TGX)
    region = jnp.concatenate([upper, lower], axis=2)
    gathered = lax.all_gather(probe.astype(jnp.bfloat16), "tile", axis=3, tiled=True)
    valid_mask = (jnp.arange(slots, dtype=jnp.int32) < tile_load[0]).astype(jnp.float32)

    def cut_patch(row_start, col_start):
        return lax.dynamic_slice(region, (0, 0, row_start, col_start), (layers, 2, width, width))

    patches = jax.vmap(cut_patch)(offsets[0], offsets[1])
    probe_pick = jnp.take(gathered, scan_of_slot, axis=0)
    wave_re = probe_pick[:, :, 0]
    wave_im = probe_pick[:, :, 1]
    incident = []
    for layer_index in range(layers):
        incident.append((wave_re, wave_im))
        next_re, next_im = complex_times(
            wave_re, wave_im, patches[:, None, layer_index, 0], patches[:, None, layer_index, 1]
        )
        wave_re = next_re.astype(jnp.bfloat16)
        wave_im = next_im.astype(jnp.bfloat16)
        if layer_index + 1 < layers:
            wave_re, wave_im = propagate(wave_re, wave_im, tables, False)
    far_re, far_im = transform(wave_re, wave_im, tables, False)
    far_re32 = far_re.astype(jnp.float32)
    far_im32 = far_im.astype(jnp.float32)
    partial_power = jnp.sum(far_re32 * far_re32 + far_im32 * far_im32, axis=1)
    power = lax.psum(partial_power, "mode")
    misfit = (power - patterns) * valid_mask[:, None, None]
    back_re = (residual_weight * misfit[:, None] * far_re32).astype(jnp.bfloat16)
    back_im = (residual_weight * misfit[:, None] * far_im32).astype(jnp.bfloat16)
    back_re, back_im = transform(back_re, back_im, tables, True)
    slice_terms = [None] * layers
    probe_terms = None
    for layer_index in reversed(range(layers)):
        inc_re, inc_im = incident[layer_index]
        grad_re, grad_im = conj_times(inc_re, inc_im, back_re, back_im)
        slice_terms[layer_index] = jnp.stack(
            [jnp.sum(grad_re, axis=1), jnp.sum(grad_im, axis=1)], axis=1
        )
        carry_re, carry_im = conj_times(
            patches[:, None, layer_index, 0], patches[:, None, layer_index, 1], back_re, back_im
        )
        if layer_index > 0:
            back_re, back_im = propagate(
                carry_re.astype(jnp.bfloat16), carry_im.astype(jnp.bfloat16), tables, True
            )
        else:
            probe_terms = jnp.stack([carry_re, carry_im], axis=2)
    slot_grads = jnp.stack(slice_terms, axis=1)
    region_grad = jnp.zeros((layers, 2, 2 * tile_side, 2 * tile_side), jnp.float32)
    for slot_index in range(slots):
        starts = (0, 0, offsets[0, slot_index], offsets[1, slot_index])
        current = lax.dynamic_slice(region_grad, starts, (layers, 2, width, width))
        region_grad = lax.dynamic_update_slice(
            region_grad, current + slot_grads[slot_index], starts
        )
    region_grad = lax.psum(region_grad.astype(jnp.bfloat16), "mode").astype(jnp.float32)
    from_above = from_behind(
        region_grad[:, :, tile_side:, :].astype(jnp.bfloat16), "tile", TGX
    ).astype(jnp.float32)
    upper_grad = region_grad[:, :, :tile_side, :] + from_above
    from_left = from_behind(upper_grad[:, :, :, tile_side:].astype(jnp.bfloat16), "tile", 1).astype(
        jnp.float32
    )
    tile_grad = upper_grad[:, :, :, :tile_side] + from_left
    scan_onehot = (scan_of_slot[:, None] == jnp.arange(scans, dtype=jnp.int32)[None, :]).astype(
        jnp.float32
    )
    probe_local = jnp.einsum(
        "cs,cmrij->smrij", scan_onehot, probe_terms, precision=lax.Precision.HIGHEST
    )
    probe_grad = lax.psum_scatter(probe_local, "tile", scatter_dimension=3, tiled=True)
    object_sum = jnp.sum(tile_grad * tile_grad) / float(mode_count)
    probe_sum = jnp.sum(probe_grad * probe_grad)
    object_total, probe_total = lax.psum((object_sum, probe_sum), ("tile", "mode"))
    object_square = object_total / float(tile_count * layers * 2 * tile_side * tile_side)
    probe_square = probe_total / float(SCAN_COUNT * MODES * 2 * width * width)
    object_direction = -tile_grad[None] + object_square / object_norm_before[0] * object_previous
    new_object = object_tiles + step_sizes[0].astype(jnp.float32) / 1024.0 * object_direction
    probe_direction = -probe_grad + probe_square / probe_norm_before[0] * probe_previous
    new_probe = probe + step_sizes[1].astype(jnp.float32) / 16384.0 * probe_direction
    return (new_object, object_direction, new_probe, probe_direction)


def solution(mesh):
    return jax.shard_map(
        body,
        mesh=mesh,
        in_specs=(
            P("tile", None, None, None, None),
            P("tile", None, None, None, None),
            P(None, "mode", None, "tile", None),
            P(None, "mode", None, "tile", None),
            P("tile", None, None),
            P(None, "tile"),
            P("tile"),
            P("tile"),
            P(),
            P(),
            P(),
        ),
        out_specs=(
            P("tile", None, None, None, None),
            P("tile", None, None, None, None),
            P(None, "mode", None, "tile", None),
            P(None, "mode", None, "tile", None),
        ),
        check_vma=False,
    )
```

profile of v0, /device:TPU:1, one launch (start us, length us, event | category | flops | bytes accessed | tf_op | source)
XLA Modules:
  0.0 1247.7 jit_solution(10554642321168706119)
XLA Ops:
  7.2 1.5 copy.264
  12.1 11.3 collective-permute-done
  25.1 1.8 fusion.154
  26.9 28.3 %collective-permute-done.1 = bf16[2,2,256,512]{3,2,1,0:T(8,128)(2,1)} collective-permute-done((bf16[2,2,256,512]{3,2,1,0:T(8,128)(2,1)S(1)}, bf16[2,2,256,512]{3,2,1,0:T(8,128)(2,1)}, u32[]{:S(2)}, u32[]{:S(2)}) %collective-permute-start.1) | collective-permute-done | bytes 1048608 | tf_op jit(solution)/shard_map/ppermute | solution.py:16
  55.2 1.4 pad_maximum_fusion
  56.6 6.0 while.1
  57.2 2.4 bitcast_dynamic-update-slice_fusion.2
  60.2 2.4 bitcast_dynamic-update-slice_fusion.2
  62.6 1.4 bitcast_convert_fusion.3
  66.4 200.3 %all-gather.2.cloned.1.call-done = bf16[4,2,2,256,256]{4,0,2,1,3:T(4,128)(2,1)} async-done(((bf16[4,2,2,4,256]{4,0,2,1,3:T(4,128)(2,1)}), bf16[4,2,2,256,256]{4,0,2,1,3:T(4,128)(2,1)}) %all-gather.2.cloned.1.call-update) | async-done | bytes 2097168 | tf_op jit(solution)/shard_map/all_gather | solution.py:100
  266.7 2.3 copy.137
  269.0 1.6 gather_fusion
  270.6 2.0 copy.138
  282.0 1.4 add_convert_fusion.3
  284.7 1.4 fusion.133
  292.4 2.4 add_convert_fusion.2
  298.7 1.7 fusion.125
  304.1 2.1 add_reduce_fusion.1
  311.9 2.1 copy.169
  317.1 82.1 %all-reduce.6.cloned.1.call-done = f32[2,256,256]{1,2,0:T(8,128)} async-done(((f32[2,256,256]{1,2,0:T(8,128)}), f32[2,256,256]{1,2,0:T(8,128)}) %all-reduce.6.cloned.1.call-update) | async-done | bytes 524304 | tf_op jit(solution)/shard_map/psum | solution.py:124
  399.3 1.3 multiply_multiply_fusion
  409.8 2.5 add_reduce_fusion
  421.2 1.4 add_convert_fusion
  423.8 1.5 fusion.109
  431.7 3.0 add_bitcast_fusion
  435.0 2.5 broadcast_in_dim.11
  437.4 11.2 dynamic_update_slice.6
  448.6 1.8 fusion.59
  450.4 12.3 dynamic_update_slice.7
  462.7 3.9 convert_element_type.598
  468.1 1.6 pad_maximum_fusion.1
  469.6 3.1 copy.197
  472.7 6.6 fusion.156
  479.4 50.8 %all-reduce.8.cloned.1.call-done = bf16[2,2,512,512]{2,3,1,0:T(8,128)(2,1)} async-done(((bf16[2,2,512,512]{2,3,1,0:T(8,128)(2,1)}), bf16[2,2,512,512]{2,3,1,0:T(8,128)(2,1)}) %all-reduce.8.cloned.1.call-update) | async-done | bytes 2097168 | tf_op jit(solution)/shard_map/psum | solution.py:154
  530.2 1.4 slice.116
  531.7 3.4 collective-permute-start.2
  535.1 22.3 %collective-permute-done.2 = bf16[2,2,256,512]{2,3,1,0:T(8,128)(2,1)S(1)} collective-permute-done((bf16[2,2,256,512]{2,3,1,0:T(8,128)(2,1)S(1)}, bf16[2,2,256,512]{2,3,1,0:T(8,128)(2,1)S(1)}, u32[]{:S(2)}, u32[]{:S(2)}) %collective-permute-start.2) | collective-permute-done | bytes 1048608 | tf_op jit(solution)/shard_map/ppermute | solution.py:16
  558.4 3.9 collective-permute-start.3
  562.4 1.3 copy.196
  566.9 2.6 copy.195
  570.8 2.8 collective-permute-done.3
  573.6 1.9 multiply_reduce_fusion
  576.2 531.9 %all-reduce.10.cloned.1.call-done = f32[4,2,2,256,256]{4,0,3,2,1:T(4,128)} async-done(((f32[4,2,2,256,256]{4,0,3,2,1:T(4,128)}), f32[4,2,2,256,256]{4,0,3,2,1:T(4,128)}) %all-reduce.10.cloned.1.call-update) | async-done | bytes 4194320
  1108.1 1.5 multiply_reduce_fusion.1
  1109.6 120.8 %all-reduce.1 = (f32[]{:T(128)}, f32[]{:T(128)}) all-reduce(f32[]{:T(128)S(6)} %div.27, f32[]{:T(128)} %multiply_reduce_fusion.1), channel_id=1, replica_groups=mesh['tile'=64,'mode'=4] {'tile','mode'}, use_global_device_ids=true, to_apply=%region_8.9 | all-reduce | flops 2 | bytes 16 | tf_op jit(solution)/shard_map/psum | solution.py:172
  1234.0 2.9 multiply_add_fusion
  1237.0 2.6 copy.200
  1239.6 1.3 copy.201
  (133 shorter events, 65.6 us)
Async XLA Ops:
  7.2 17.8 %copy-start.23 = (s32[2]{0:T(128)S(1)}, s32[2]{0:T(128)}, u32[]{:S(2)}) copy-start(s32[2]{0:T(128)} %param.17) | copy-start | bytes 28
  7.2 259.5 %all-gather.2.cloned.1.call-start = ((), (), s32[]{:S(2)}) async-start(), calls=%async_computation | async-start | bytes 2129920 | tf_op jit(solution)/shard_map/all_gather | solution.py:100
  8.7 390.5 %all-reduce.6.cloned.1.call-start = ((), (), s32[]{:S(2)}) async-start(), calls=%async_computation.1 | async-start | bytes 1048576 | tf_op jit(solution)/shard_map/psum | solution.py:124
  10.1 13.3 %collective-permute-start = (bf16[2,2,256,256]{3,2,1,0:T(8,128)(2,1)S(1)}, bf16[2,2,256,256]{3,2,1,0:T(8,128)(2,1)S(1)}, u32[]{:S(2)}, u32[]{:S(2)}) collective-permute-start(bf16[2,2,256,256]{3,2,1,0:T(8,128)(2,1)S(1)} %convert_bitcast_fusion), channel_id=1, source_target_pairs={{4,0},{8,4},{12,8},{16,12},{20,16},{24,20},{28,24},{32,28},{36,32}... | collective-permute-start | bytes 1572872 | tf_op jit(solution)/shard_map/ppermute | solution.py:16
  23.5 31.7 %collective-permute-start.1 = (bf16[2,2,256,512]{3,2,1,0:T(8,128)(2,1)S(1)}, bf16[2,2,256,512]{3,2,1,0:T(8,128)(2,1)}, u32[]{:S(2)}, u32[]{:S(2)}) collective-permute-start(bf16[2,2,256,512]{3,2,1,0:T(8,128)(2,1)S(1)} %pad_maximum_fusion.3), channel_id=1, source_target_pairs={{32,0},{36,4},{40,8},{44,12},{48,16},{52,20},{56,24},{60,28},{64,3... | collective-permute-start | bytes 3145736 | tf_op jit(solution)/shard_map/ppermute | solution.py:16
  64.2 208.5 %copy-start.2 = (f32[2,256,256]{1,2,0:T(8,128)}, f32[2,256,256]{1,2,0:T(8,128)S(1)}, u32[]{:S(2)}) copy-start(f32[2,256,256]{1,2,0:T(8,128)S(1)} %copy.142) | copy-start | bytes 1572868
  64.4 208.3 %copy-start.4 = (f32[2,256,256]{1,2,0:T(8,128)}, f32[2,256,256]{1,2,0:T(8,128)S(1)}, u32[]{:S(2)}) copy-start(f32[2,256,256]{1,2,0:T(8,128)S(1)} %copy.143) | copy-start | bytes 1572868
  272.8 1.6 copy-start
  279.4 2.5 copy-start.18
  289.9 2.5 copy-start.6
  289.9 2.5 copy-start.8
  304.1 2.2 copy-start.21
  306.3 224.0 %all-reduce.8.cloned.1.call-start = ((), (), s32[]{:S(2)}) async-start(), calls=%async_computation.2 | async-start | bytes 4194304 | tf_op jit(solution)/shard_map/psum | solution.py:154
  408.3 1.3 copy-start.7
  408.3 1.3 copy-start.9
  408.3 1.5 copy-start.11
  418.6 2.5 copy-start.17
  429.1 2.6 copy-start.1
  429.1 2.6 copy-start.3
  429.1 2.6 copy-start.5
  466.5 1.2 copy-start.12
  466.5 1.5 copy-start.13
  466.6 641.5 %all-reduce.10.cloned.1.call-start = ((), (), s32[]{:S(2)}) async-start(), calls=%async_computation.3 | async-start | bytes 8388608
  530.2 27.1 %copy-start.16 = (bf16[2,2,512,512]{2,3,1,0:T(8,128)(2,1)S(1)}, bf16[2,2,512,512]{2,3,1,0:T(8,128)(2,1)}, u32[]{:S(2)}) copy-start(bf16[2,2,512,512]{2,3,1,0:T(8,128)(2,1)} %all-reduce.8.cloned.1.call-done) | copy-start | bytes 6291460
  531.7 30.7 %copy-start.10 = (f32[1,2,2,256,256]{4,3,2,1,0:T(8,128)S(1)}, f32[1,2,2,256,256]{4,3,2,1,0:T(8,128)}, u32[]{:S(2)}) copy-start(f32[1,2,2,256,256]{4,3,2,1,0:T(8,128)} %param.11) | copy-start | bytes 3145732
  531.7 25.6 %collective-permute-start.2 = (bf16[2,2,256,512]{2,3,1,0:T(8,128)(2,1)S(1)}, bf16[2,2,256,512]{2,3,1,0:T(8,128)(2,1)S(1)}, u32[]{:S(2)}, u32[]{:S(2)}) collective-permute-start(bf16[2,2,256,512]{2,3,1,0:T(8,128)(2,1)S(1)} %slice.116), channel_id=1, source_target_pairs={{0,32},{4,36},{8,40},{12,44},{16,48},{20,52},{24,56},{28,60},{32,6... | collective-permute-start | bytes 3145736 | tf_op jit(solution)/shard_map/ppermute | solution.py:16
  557.5 6.8 copy-start.22
  558.4 15.2 %collective-permute-start.3 = (bf16[2,2,256,256]{2,3,1,0:T(8,128)(2,1)}, bf16[2,2,256,256]{2,3,1,0:T(8,128)(2,1)}, u32[]{:S(2)}, u32[]{:S(2)}) collective-permute-start(bf16[2,2,256,256]{2,3,1,0:T(8,128)(2,1)} %slice.159), channel_id=1, source_target_pairs={{0,4},{4,8},{8,12},{12,16},{16,20},{20,24},{24,28},{28,32},{32,36}... | collective-permute-start | bytes 1572872 | tf_op jit(solution)/shard_map/ppermute | solution.py:16
  562.4 7.2 copy-start.24
  563.7 667.4 %copy-start.19 = (f32[4,2,2,4,256]{4,3,2,1,0:T(4,128)S(1)}, f32[4,2,2,4,256]{4,3,2,1,0:T(4,128)}, u32[]{:S(2)}) copy-start(f32[4,2,2,4,256]{4,3,2,1,0:T(4,128)} %param.13) | copy-start | bytes 196612
  563.7 667.4 %copy-start.20 = (f32[4,2,2,4,256]{4,3,2,1,0:T(4,128)S(1)}, f32[4,2,2,4,256]{4,3,2,1,0:T(4,128)}, u32[]{:S(2)}) copy-start(f32[4,2,2,4,256]{4,3,2,1,0:T(4,128)} %param.14) | copy-start | bytes 196612
  566.9 667.1 %copy-start.14 = (f32[1,2,2,256,256]{3,4,2,1,0:T(8,128)S(1)}, f32[1,2,2,256,256]{3,4,2,1,0:T(8,128)}, u32[]{:S(2)}) copy-start(f32[1,2,2,256,256]{3,4,2,1,0:T(8,128)} %copy.196) | copy-start | bytes 3145732
  1237.0 2.6 copy-start.15
Sparse Core Ops, SparseCore 0:
  10.3 256.2 all-gather.1
  306.4 92.8 all-reduce.5
  466.7 63.5 all-reduce.7
  532.7 575.3 all-reduce.9
where the time goes:
time: 1250 us
  waiting for transfers between devices  930 us (74%)
  blocking collectives  121 us (10%)
  matrix products  73.2 us (6%)
  local copies, waits for them, and re-layouts  62.1 us (5%)
  between operations  28.2 us (2%)
  other arithmetic  23.5 us (2%)
    unnamed x5, waiting for transfers between devices  532 us
    all_gather x1, waiting for transfers between devices, body(): lax.all_gather(probe.astype(jnp.bfloat16), 'tile', axis=3, tiled=True)  200 us
    psum x1, blocking collectives, body(): lax.psum((object_sum, probe_sum), ('tile', 'mode'))  121 us
    psum x1, waiting for transfers between devices, body(): power = lax.psum(partial_power, 'mode')  82.1 us
    ppermute x4, waiting for transfers between devices, from_behind(): return lax.ppermute(block, axis, route)  64.6 us
    psum x1, waiting for transfers between devices, body(): lax.psum(region_grad.astype(jnp.bfloat16), 'mode').astype(jnp.float32)  50.8 us
    dot_general x24, matrix products, left_product(): jnp.einsum('ij,...jl->...il', table, right_data, preferred_element_type=j...  35.8 us
    dot_general x24, matrix products, right_product(): jnp.einsum('...jk,kl->...jl', left_data, table, preferred_element_type=jn...  30.7 us
  transfers between devices with their start and end apart: 8, of which 8 were waited for; matrix products, arithmetic and copies ran while one was open for 3% of the time, Pallas kernels for 0%

commit v1 on v0

--- a/solution.py
+++ b/solution.py
@@ -97,7 +97,12 @@
     upper = jnp.concatenate([own_tile, east_part], axis=3)
     lower = from_behind(upper, "tile", -TGX)
     region = jnp.concatenate([upper, lower], axis=2)
-    gathered = lax.all_gather(probe.astype(jnp.bfloat16), "tile", axis=3, tiled=True)
+    gathered = jnp.concatenate(
+        lax.all_to_all(
+            jnp.stack([probe.astype(jnp.bfloat16)] * lax.axis_size("tile")), "tile", 0, 0
+        ),
+        axis=3,
+    )
     valid_mask = (jnp.arange(slots, dtype=jnp.int32) < tile_load[0]).astype(jnp.float32)
 
     def cut_patch(row_start, col_start):

time: 1250 us -> 1070 us (0.86)
  waiting for transfers between devices: 930 us -> 725 us
  starting transfers between devices: 10.1 us -> 23.9 us
    all_gather x1 -> x0, waiting for transfers between devices: 200 us -> none  [body(): lax.all_gather(probe.astype(jnp.bfloat16), 'tile', axis=3, tiled=True)]
    psum x1, waiting for transfers between devices: 82.1 us -> 42.2 us  [body(): power = lax.psum(partial_power, 'mode')]
    ppermute x4, waiting for transfers between devices: 64.6 us -> 101 us  [from_behind(): return lax.ppermute(block, axis, route)]
    all_to_all x0 -> x1, starting transfers between devices: none -> 13.9 us  [body(): lax.all_to_all(jnp.stack([probe.astype(jnp.bfloat16)] * lax.axis_size('ti...]
    unnamed x5 -> x4, waiting for transfers between devices: 532 us -> 532 us
  transfers between devices with their start and end apart: 8 -> 8, of which waited for: 8 -> 7; matrix products, arithmetic and copies ran while one was open for 3% -> 3% of each run, Pallas kernels for 0% -> 0%
where the time goes in v1:
time: 1070 us; the launch traced here: 1060 us
  waiting for transfers between devices  725 us (68%)
  blocking collectives  121 us (11%)
  matrix products  73.2 us (7%)
  local copies, waits for them, and re-layouts  65 us (6%)
  between operations  28.3 us (3%)
  starting transfers between devices  23.9 us (2%)
  other arithmetic  22.4 us (2%)
    unnamed x4, waiting for transfers between devices  532 us
    psum x1, blocking collectives, body(): lax.psum((object_sum, probe_sum), ('tile', 'mode'))  121 us
    ppermute x4, waiting for transfers between devices, from_behind(): return lax.ppermute(block, axis, route)  101 us
    psum x1, waiting for transfers between devices, body(): lax.psum(region_grad.astype(jnp.bfloat16), 'mode').astype(jnp.float32)  50.8 us
    psum x1, waiting for transfers between devices, body(): power = lax.psum(partial_power, 'mode')  42.2 us
    dot_general x24, matrix products, left_product(): jnp.einsum('ij,...jl->...il', table, right_data, preferred_element_type=j...  35.8 us
    dot_general x24, matrix products, right_product(): jnp.einsum('...jk,kl->...jl', left_data, table, preferred_element_type=jn...  30.7 us
    dynamic_update_slice x2, local copies, waits for them, and re-layouts, body(): lax.dynamic_update_slice(region_grad, current + slot_grads[slot_index], s...  23.4 us
  transfers between devices with their start and end apart: 8, of which 7 were waited for; matrix products, arithmetic and copies ran while one was open for 3% of the time, Pallas kernels for 0%

profile of v1, /device:TPU:1, one launch (start us, length us, event | category | flops | bytes accessed | tf_op | source)
XLA Modules:
  0.0 1058.7 jit_solution(7360482638565728733)
XLA Ops:
  8.1 3.3 stack.26
  11.4 13.9 %all-to-all-start = ((bf16[64,4,2,2,4,256]{5,3,4,2,1,0:T(2,128)(2,1)}), bf16[64,4,2,2,4,256]{5,3,4,2,1,0:T(2,128)(2,1)}, u32[]{:S(2)}, u32[]{:S(2)}) async-start(bf16[64,4,2,2,4,256]{5,3,4,2,1,0:T(2,128)(2,1)} %stack.26), calls=%async_computation | async-start | bytes 4194304 | tf_op jit(solution)/shard_map/all_to_all | solution.py:101
  26.7 23.5 %collective-permute-done = bf16[2,2,256,256]{3,2,1,0:T(8,128)(2,1)S(1)} collective-permute-done((bf16[2,2,256,256]{3,2,1,0:T(8,128)(2,1)S(1)}, bf16[2,2,256,256]{3,2,1,0:T(8,128)(2,1)S(1)}, u32[]{:S(2)}, u32[]{:S(2)}) %collective-permute-start) | collective-permute-done | bytes 524320 | tf_op jit(solution)/shard_map/ppermute | solution.py:16
  51.9 1.8 fusion.154
  53.8 51.9 %collective-permute-done.1 = bf16[2,2,256,512]{3,2,1,0:T(8,128)(2,1)} collective-permute-done((bf16[2,2,256,512]{3,2,1,0:T(8,128)(2,1)S(1)}, bf16[2,2,256,512]{3,2,1,0:T(8,128)(2,1)}, u32[]{:S(2)}, u32[]{:S(2)}) %collective-permute-start.1) | collective-permute-done | bytes 1048608 | tf_op jit(solution)/shard_map/ppermute | solution.py:16
  105.7 1.4 pad_maximum_fusion
  107.1 6.0 while.1
  107.7 2.4 bitcast_dynamic-update-slice_fusion.2
  110.7 2.4 bitcast_dynamic-update-slice_fusion.2
  113.1 1.4 bitcast_convert_fusion.3
  116.9 3.0 copy.139
  120.3 1.6 gather_fusion
  121.9 2.0 copy.141
  133.3 1.4 add_convert_fusion.3
  136.0 1.4 fusion.133
  143.8 2.4 add_convert_fusion.2
  150.0 1.7 fusion.125
  155.4 2.1 add_reduce_fusion.1
  163.2 2.1 copy.172
  168.4 42.2 %all-reduce.6.cloned.1.call-done = f32[2,256,256]{1,2,0:T(8,128)} async-done(((f32[2,256,256]{1,2,0:T(8,128)}), f32[2,256,256]{1,2,0:T(8,128)}) %all-reduce.6.cloned.1.call-update) | async-done | bytes 524304 | tf_op jit(solution)/shard_map/psum | solution.py:129
  210.6 1.3 multiply_multiply_fusion
  221.2 2.5 add_reduce_fusion
  232.5 1.4 add_convert_fusion
  235.2 1.5 fusion.109
  243.0 3.0 add_bitcast_fusion
  246.3 2.5 broadcast_in_dim.11
  248.8 11.2 %dynamic_update_slice.6 = f32[2,2,512,512]{2,3,1,0:T(8,128)} dynamic-update-slice(f32[2,2,512,512]{2,3,1,0:T(8,128)} %broadcast_in_dim.11, f32[2,2,256,256]{2,3,1,0:T(8,128)S(1)} %fusion.57, s32[]{:T(128)} %constant.27.clone.1, s32[]{:T(128)} %constant.27.clone.1, s32[]{:T(128)S(6)} %select_n.176, s32[]{:T(128)S(6)} %select_n.177) | dynamic-update-slice | bytes 2097156 | tf_op jit(solution)/shard_map/dynamic_update_slice | solution.py:156
  259.9 1.8 fusion.59
  261.7 12.3 %dynamic_update_slice.7 = f32[2,2,512,512]{2,3,1,0:T(8,128)} dynamic-update-slice(f32[2,2,512,512]{2,3,1,0:T(8,128)} %dynamic_update_slice.6, f32[2,2,256,256]{2,3,1,0:T(8,128)S(1)} %fusion.59, s32[]{:T(128)} %constant.27.clone.1, s32[]{:T(128)} %constant.27.clone.1, s32[]{:T(128)S(6)} %select_n.178, s32[]{:T(128)S(6)} %select_n.179) | dynamic-update-slice | bytes 2097156 | tf_op jit(solution)/shard_map/dynamic_update_slice | solution.py:156
  274.0 3.9 convert_element_type.598
  279.4 1.6 pad_maximum_fusion.1
  281.0 3.1 copy.200
  284.1 6.6 fusion.156
  290.7 50.8 %all-reduce.8.cloned.1.call-done = bf16[2,2,512,512]{2,3,1,0:T(8,128)(2,1)} async-done(((bf16[2,2,512,512]{2,3,1,0:T(8,128)(2,1)}), bf16[2,2,512,512]{2,3,1,0:T(8,128)(2,1)}) %all-reduce.8.cloned.1.call-update) | async-done | bytes 2097168 | tf_op jit(solution)/shard_map/psum | solution.py:159
  341.5 1.4 slice.116
  343.0 3.4 collective-permute-start.2
  346.4 22.3 %collective-permute-done.2 = bf16[2,2,256,512]{2,3,1,0:T(8,128)(2,1)S(1)} collective-permute-done((bf16[2,2,256,512]{2,3,1,0:T(8,128)(2,1)S(1)}, bf16[2,2,256,512]{2,3,1,0:T(8,128)(2,1)S(1)}, u32[]{:S(2)}, u32[]{:S(2)}) %collective-permute-start.2) | collective-permute-done | bytes 1048608 | tf_op jit(solution)/shard_map/ppermute | solution.py:16
  369.7 3.9 collective-permute-start.3
  373.7 1.3 copy.199
  378.2 2.6 copy.198
  382.1 2.9 collective-permute-done.3
  385.0 1.9 multiply_reduce_fusion
  387.5 531.6 %all-reduce.10.cloned.1.call-done = f32[4,2,2,256,256]{4,0,3,2,1:T(4,128)} async-done(((f32[4,2,2,256,256]{4,0,3,2,1:T(4,128)}), f32[4,2,2,256,256]{4,0,3,2,1:T(4,128)}) %all-reduce.10.cloned.1.call-update) | async-done | bytes 4194320
  919.1 1.5 multiply_reduce_fusion.1
  920.6 120.8 %all-reduce.1 = (f32[]{:T(128)}, f32[]{:T(128)}) all-reduce(f32[]{:T(128)S(6)} %div.27, f32[]{:T(128)} %multiply_reduce_fusion.1), channel_id=1, replica_groups=mesh['tile'=64,'mode'=4] {'tile','mode'}, use_global_device_ids=true, to_apply=%region_8.9 | all-reduce | flops 2 | bytes 16 | tf_op jit(solution)/shard_map/psum | solution.py:177
  1045.1 2.9 multiply_add_fusion
  1048.0 2.6 copy.203
  1050.6 1.3 copy.204
  (137 shorter events, 64.7 us)
Async XLA Ops:
  11.4 14.0 %copy-start.10 = (f32[1,2,2,256,256]{4,3,2,1,0:T(8,128)S(1)}, f32[1,2,2,256,256]{4,3,2,1,0:T(8,128)}, u32[]{:S(2)}) copy-start(f32[1,2,2,256,256]{4,3,2,1,0:T(8,128)} %param.11) | copy-start | bytes 3145732
  11.4 15.3 %copy-start.22 = (s32[2,2]{1,0:T(2,128)S(1)}, s32[2,2]{1,0:T(2,128)}, u32[]{:S(2)}) copy-start(s32[2,2]{1,0:T(2,128)} %param.16) | copy-start | bytes 52
  11.4 105.5 %all-to-all-start = ((bf16[64,4,2,2,4,256]{5,3,4,2,1,0:T(2,128)(2,1)}), bf16[64,4,2,2,4,256]{5,3,4,2,1,0:T(2,128)(2,1)}, u32[]{:S(2)}, u32[]{:S(2)}) async-start(bf16[64,4,2,2,4,256]{5,3,4,2,1,0:T(2,128)(2,1)} %stack.26), calls=%async_computation | async-start | bytes 4194304 | tf_op jit(solution)/shard_map/all_to_all | solution.py:101
  25.3 26.5 %copy-start.24 = (s32[2]{0:T(128)S(1)}, s32[2]{0:T(128)}, u32[]{:S(2)}) copy-start(s32[2]{0:T(128)} %param.17) | copy-start | bytes 28
  25.3 185.3 %all-reduce.6.cloned.1.call-start = ((), (), s32[]{:S(2)}) async-start(), calls=%async_computation.1 | async-start | bytes 1048576 | tf_op jit(solution)/shard_map/psum | solution.py:129
  25.4 24.8 %collective-permute-start = (bf16[2,2,256,256]{3,2,1,0:T(8,128)(2,1)S(1)}, bf16[2,2,256,256]{3,2,1,0:T(8,128)(2,1)S(1)}, u32[]{:S(2)}, u32[]{:S(2)}) collective-permute-start(bf16[2,2,256,256]{3,2,1,0:T(8,128)(2,1)S(1)} %convert_bitcast_fusion), channel_id=1, source_target_pairs={{4,0},{8,4},{12,8},{16,12},{20,16},{24,20},{28,24},{32,28},{36,32}... | collective-permute-start | bytes 1572872 | tf_op jit(solution)/shard_map/ppermute | solution.py:16
  50.3 55.4 %collective-permute-start.1 = (bf16[2,2,256,512]{3,2,1,0:T(8,128)(2,1)S(1)}, bf16[2,2,256,512]{3,2,1,0:T(8,128)(2,1)}, u32[]{:S(2)}, u32[]{:S(2)}) collective-permute-start(bf16[2,2,256,512]{3,2,1,0:T(8,128)(2,1)S(1)} %pad_maximum_fusion.3), channel_id=1, source_target_pairs={{32,0},{36,4},{40,8},{44,12},{48,16},{52,20},{56,24},{60,28},{64,3... | collective-permute-start | bytes 3145736 | tf_op jit(solution)/shard_map/ppermute | solution.py:16
  114.6 9.4 copy-start.2
  114.9 9.2 copy-start.4
  124.1 1.6 copy-start
  130.8 2.5 copy-start.19
  141.2 2.5 copy-start.6
  141.2 2.5 copy-start.8
  157.5 184.0 %all-reduce.8.cloned.1.call-start = ((), (), s32[]{:S(2)}) async-start(), calls=%async_computation.2 | async-start | bytes 4194304 | tf_op jit(solution)/shard_map/psum | solution.py:159
  219.6 1.3 copy-start.7
  219.6 1.3 copy-start.9
  219.6 1.5 copy-start.12
  230.0 2.5 copy-start.18
  240.4 2.6 copy-start.1
  240.4 2.6 copy-start.3
  240.5 2.6 copy-start.5
  277.9 1.2 copy-start.13
  277.9 1.5 copy-start.14
  277.9 641.2 %all-reduce.10.cloned.1.call-start = ((), (), s32[]{:S(2)}) async-start(), calls=%async_computation.3 | async-start | bytes 8388608
  341.5 27.1 %copy-start.17 = (bf16[2,2,512,512]{2,3,1,0:T(8,128)(2,1)S(1)}, bf16[2,2,512,512]{2,3,1,0:T(8,128)(2,1)}, u32[]{:S(2)}) copy-start(bf16[2,2,512,512]{2,3,1,0:T(8,128)(2,1)} %all-reduce.8.cloned.1.call-done) | copy-start | bytes 6291460
  343.0 30.7 %copy-start.11 = (f32[1,2,2,256,256]{4,3,2,1,0:T(8,128)S(1)}, f32[1,2,2,256,256]{4,3,2,1,0:T(8,128)}, u32[]{:S(2)}) copy-start(f32[1,2,2,256,256]{4,3,2,1,0:T(8,128)} %param.11) | copy-start | bytes 3145732
  343.0 25.6 %collective-permute-start.2 = (bf16[2,2,256,512]{2,3,1,0:T(8,128)(2,1)S(1)}, bf16[2,2,256,512]{2,3,1,0:T(8,128)(2,1)S(1)}, u32[]{:S(2)}, u32[]{:S(2)}) collective-permute-start(bf16[2,2,256,512]{2,3,1,0:T(8,128)(2,1)S(1)} %slice.116), channel_id=1, source_target_pairs={{0,32},{4,36},{8,40},{12,44},{16,48},{20,52},{24,56},{28,60},{32,6... | collective-permute-start | bytes 3145736 | tf_op jit(solution)/shard_map/ppermute | solution.py:16
  368.8 6.8 copy-start.23
  369.7 15.3 %collective-permute-start.3 = (bf16[2,2,256,256]{2,3,1,0:T(8,128)(2,1)}, bf16[2,2,256,256]{2,3,1,0:T(8,128)(2,1)}, u32[]{:S(2)}, u32[]{:S(2)}) collective-permute-start(bf16[2,2,256,256]{2,3,1,0:T(8,128)(2,1)} %slice.159), channel_id=1, source_target_pairs={{0,4},{4,8},{8,12},{12,16},{16,20},{20,24},{24,28},{28,32},{32,36}... | collective-permute-start | bytes 1572872 | tf_op jit(solution)/shard_map/ppermute | solution.py:16
  373.7 7.2 copy-start.25
  375.0 667.1 %copy-start.20 = (f32[4,2,2,4,256]{4,3,2,1,0:T(4,128)S(1)}, f32[4,2,2,4,256]{4,3,2,1,0:T(4,128)}, u32[]{:S(2)}) copy-start(f32[4,2,2,4,256]{4,3,2,1,0:T(4,128)} %param.13) | copy-start | bytes 196612
  375.0 667.1 %copy-start.21 = (f32[4,2,2,4,256]{4,3,2,1,0:T(4,128)S(1)}, f32[4,2,2,4,256]{4,3,2,1,0:T(4,128)}, u32[]{:S(2)}) copy-start(f32[4,2,2,4,256]{4,3,2,1,0:T(4,128)} %param.14) | copy-start | bytes 196612
  378.2 666.9 %copy-start.15 = (f32[1,2,2,256,256]{3,4,2,1,0:T(8,128)S(1)}, f32[1,2,2,256,256]{3,4,2,1,0:T(8,128)}, u32[]{:S(2)}) copy-start(f32[1,2,2,256,256]{3,4,2,1,0:T(8,128)} %copy.199) | copy-start | bytes 3145732
  1048.0 2.6 copy-start.16
Sparse Core Ops, SparseCore 0:
  157.7 52.8 all-reduce.5
  278.0 63.4 all-reduce.7
  344.2 574.9 all-reduce.9
